TPU v7x, 32 devices: a whole 2x2x4 slice. The times are simulated.
32 devices in a mesh: groups: 2 (over y), people: 4 (over z), blocks: 2 (over x), sub: 2 (over core).
Axes of the slice: x: 2, y: 2, z: 4, core: 2. Of those that a mesh axis runs over, the one named last changes fastest.
Arguments:
- dosage: int32 [4096, 2048], P(('groups', 'people', 'sub'), 'blocks'), parts along dimension 0, may hold values from 0 to 200
- fold: int32 [4096], P(('groups', 'people', 'sub')), parts along dimension 0, may hold values from 0 to 1, as said below
- pheno: bfloat16 [4096, 48], P(('groups', 'people', 'sub')), parts along dimension 0, may hold values from -8 to 8
- ridges: float32 [5], replicated, may hold values from 1 to 20
Outputs:
- second: float32 [48, 5, 4096], P(('blocks', 'sub'), None, ('groups', 'people')), parts along dimension 2
There are 2 independent parts, one for each index of `groups`. A program takes and returns all parts, laid end to end along the dimension named above; an argument that names none is the same for every part. Nothing has to cross between parts.
Inputs may be any that keep to these rules, and one draw needn't show every extreme that they name: Each fold holds exactly 1024 people.
All inputs are finite; a program needn't handle non-finite values.
Results may differ from a plain program's by a relative error of at most 0.0021.
Values may be sent and summed in bfloat16 or wider, within the bound.
No kernel may reach another device: no remote copies, remote signals or barrier semaphores. Data moves between devices by JAX's collectives and lax.ppermute only.
A program may use at most 64 MiB of HBM per device.

v0:
```python
import jax
import jax.numpy as jnp
from jax import lax
from jax.sharding import PartitionSpec as P

TRAITS = 48
RIDGES = 5
FOLDS = 2
ITERS = 10
ITERS_TWO = 4
highest = lax.Precision.HIGHEST


def conjugate(apply_system, right_side, steps):
    estimate = jnp.zeros_like(right_side)
    residual = right_side
    direction = right_side
    current = jnp.sum(residual * residual, -2, keepdims=True)
    for step in range(steps):
        image = apply_system(direction)
        alpha = current / jnp.sum(direction * image, -2, keepdims=True)
        estimate = estimate + alpha * direction
        residual = residual - alpha * image
        following = jnp.sum(residual * residual, -2, keepdims=True)
        direction = residual + following / current * direction
        current = following
    return estimate


def covariance_rows(gram_rows, row_sums, all_sums, row_mean, all_mean, train_count):
    return (
        gram_rows
        - row_sums[:, None] * all_mean[None, :]
        - row_mean[:, None] * all_sums[None, :]
        + train_count * row_mean[:, None] * all_mean[None, :]
    )


def train_total(pieces, fold_index):
    return sum([pieces[other] for other in range(FOLDS) if other != fold_index])


def system_rows(shares, sums_all, column_mean, column_spread, row_start, share_rows, train_count):
    row_mean = lax.dynamic_slice_in_dim(column_mean, row_start, share_rows, 0)
    row_spread = lax.dynamic_slice_in_dim(column_spread, row_start, share_rows, 0)
    systems = []
    for fold_index in range(FOLDS):
        sums_train = train_total(sums_all, fold_index)
        row_sums = lax.dynamic_slice_in_dim(sums_train, row_start, share_rows, 0)
        covariance = covariance_rows(
            train_total(shares, fold_index),
            row_sums,
            sums_train,
            row_mean,
            column_mean,
            train_count,
        )
        systems.append(covariance / (train_count * row_spread[:, None] * column_spread[None, :]))
    return (jnp.stack(systems), row_spread)


def shards(dosage, fold, pheno, ridges):
    row_count, block_size = dosage.shape
    people_count = lax.axis_size("people")
    sub_count = lax.axis_size("sub")
    people = row_count * people_count * sub_count
    train_count = people - people // FOLDS
    centred = (dosage - 100).astype(jnp.bfloat16)
    pheno_wide = pheno.astype(jnp.float32)
    masks = [fold[:, None] == fold_index for fold_index in range(FOLDS)]
    grams, sums, squares, cross, totals = ([], [], [], [], [])
    for mask in masks:
        masked = jnp.where(mask, centred, jnp.zeros_like(centred))
        grams.append(
            lax.dot_general(
                masked, centred, (((0,), (0,)), ((), ())), preferred_element_type=jnp.float32
            )
        )
        masked_wide = masked.astype(jnp.float32)
        sums.append(jnp.sum(masked_wide, 0))
        squares.append(jnp.sum(masked_wide * masked_wide, 0))
        cross.append(
            lax.dot_general(
                masked, pheno, (((0,), (0,)), ((), ())), preferred_element_type=jnp.float32
            )
        )
        totals.append(jnp.sum(jnp.where(mask, pheno_wide, 0.0), 0))
    sums_all, squares_all, cross_all, totals_all = lax.psum(
        (jnp.stack(sums), jnp.stack(squares), jnp.stack(cross), jnp.stack(totals)),
        ("people", "sub"),
    )
    column_mean = sum([sums_all[fold_index] for fold_index in range(FOLDS)]) / people
    column_spread = jnp.sqrt(
        sum([squares_all[fold_index] for fold_index in range(FOLDS)]) / people
        - column_mean * column_mean
        + 1e-05
    )
    right_sides = []
    for fold_index in range(FOLDS):
        right_sides.append(
            (
                train_total(cross_all, fold_index)
                - column_mean[:, None] * train_total(totals_all, fold_index)[None, :]
            )
            / (train_count * column_spread[:, None])
        )
    gram_stack = jnp.stack(grams)
    share_rows = block_size // (people_count * sub_count)
    row_start = (lax.axis_index("people") * sub_count + lax.axis_index("sub")) * share_rows
    shares = lax.psum_scatter(gram_stack, ("people", "sub"), scatter_dimension=1, tiled=True)
    systems, row_spread = system_rows(
        shares, sums_all, column_mean, column_spread, row_start, share_rows, train_count
    )
    whole = lax.all_gather(systems, ("people", "sub"), axis=1, tiled=True)
    own_fold = lax.axis_index("sub")
    system = lax.dynamic_index_in_dim(whole, own_fold, 0, keepdims=False)
    trait_share = TRAITS // people_count
    trait_start = lax.axis_index("people") * trait_share
    right_own = lax.dynamic_index_in_dim(jnp.stack(right_sides), own_fold, 0, keepdims=False)
    right_cols = lax.dynamic_slice_in_dim(right_own, trait_start, trait_share, 1)
    shifts = jnp.repeat(ridges, trait_share)
    estimate = conjugate(
        lambda direction: jnp.dot(system, direction, precision=highest) + shifts * direction,
        jnp.tile(right_cols, (1, RIDGES)),
        ITERS,
    )
    scaled = (estimate / column_spread[:, None]).astype(jnp.bfloat16)
    scaled = scaled.reshape(block_size, RIDGES, trait_share)
    gathered = lax.all_gather(scaled[None], ("people", "sub"), axis=0, tiled=True)
    coefficients = gathered.reshape(people_count, sub_count, block_size, RIDGES, trait_share)
    coefficients = coefficients.transpose(1, 2, 3, 0, 4).reshape(FOLDS, block_size, RIDGES * TRAITS)
    prediction = jnp.zeros((row_count, RIDGES * TRAITS), jnp.float32)
    for fold_index in range(FOLDS):
        offset = jnp.dot(
            column_mean, coefficients[fold_index].astype(jnp.float32), precision=highest
        )
        outcome = (
            jnp.dot(centred, coefficients[fold_index], preferred_element_type=jnp.float32) - offset
        )
        prediction = prediction + jnp.where(masks[fold_index], outcome, 0.0)
    prediction = prediction.astype(jnp.bfloat16).reshape(1, row_count, RIDGES, TRAITS)
    moved, moved_pheno = (
        lax.all_to_all(prediction, ("blocks", "sub"), split_axis=3, concat_axis=0, tiled=True),
        lax.all_to_all(
            pheno[None, :, None, :], ("blocks", "sub"), split_axis=3, concat_axis=0, tiled=True
        ),
    )
    block_count = lax.axis_size("blocks")
    trait_group = TRAITS // (block_count * sub_count)
    predictors = moved.reshape(block_count, sub_count, row_count, RIDGES, trait_group)
    predictors = predictors.transpose(1, 2, 4, 0, 3).reshape(
        sub_count * row_count, trait_group, block_count * RIDGES
    )
    targets = moved_pheno.reshape(block_count, sub_count, row_count, trait_group)[0]
    targets = targets.reshape(sub_count * row_count, trait_group)
    gram_two = jnp.einsum(
        "nta,ntb->tab", predictors, predictors, preferred_element_type=jnp.float32
    )
    cross_two = jnp.einsum("nt,nta->ta", targets, predictors, preferred_element_type=jnp.float32)
    gram_two, cross_two = lax.psum((gram_two, cross_two), "people")
    gram_two = gram_two / people
    cross_two = cross_two / people
    predictor_count = block_count * RIDGES
    level = jnp.trace(gram_two, axis1=1, axis2=2) / predictor_count + 1e-06
    level_shift = ridges[None, None, :] * level[:, None, None]
    right_two = jnp.broadcast_to(cross_two[:, :, None], (trait_group, predictor_count, RIDGES))
    weights = conjugate(
        lambda direction: jnp.einsum("tab,tbr->tar", gram_two, direction, precision=highest)
        + level_shift * direction,
        right_two,
        ITERS_TWO,
    )
    return jnp.einsum("nta,tar->trn", predictors.astype(jnp.float32), weights, precision=highest)


def solution(mesh):
    return jax.shard_map(
        shards,
        mesh=mesh,
        in_specs=(
            P(("groups", "people", "sub"), "blocks"),
            P(("groups", "people", "sub")),
            P(("groups", "people", "sub"), None),
            P(),
        ),
        out_specs=P(("blocks", "sub"), None, ("groups", "people")),
        check_vma=False,
    )
```

profile of v0, /device:TPU:0, one launch (start us, length us, event | category | flops | bytes accessed | tf_op | source)
XLA Modules:
  0.0 376.7 jit_solution(10997729040896676900)
XLA Ops:
  6.5 0.7 broadcast_compare_fusion
  7.2 1.7 convert_reduce_fusion.1
  8.9 0.8 convolution_bitcast_fusion
  9.7 0.8 convolution_bitcast_fusion.1
  10.6 4.1 %pad_maximum_fusion = f32[2,1024,1024]{2,1,0:T(8,128)} fusion(f32[1,1024,1024]{2,1,0:T(8,128)S(1)} %convolution_bitcast_fusion, f32[1,1024,1024]{2,1,0:T(8,128)S(1)} %convolution_bitcast_fusion.1), kind=kLoop, calls=%fused_computation | loop fusion | flops 2097152 | bytes 16777216 | tf_op jit(solution)/shard_map/stack | solution.py:107
  14.7 0.6 copy-done
  15.9 0.8 pad_maximum_fusion.2
  17.0 31.8 %all-reduce = (f32[2,1024]{1,0:T(2,128)S(1)}, f32[2,1024]{1,0:T(2,128)S(1)}, f32[2,48]{1,0:T(2,128)S(1)}) all-reduce(f32[2,1024]{1,0:T(2,128)S(1)} %get-tuple-element.88, f32[2,1024]{1,0:T(2,128)S(1)} %get-tuple-element.87, f32[2,48]{1,0:T(2,128)S(1)} %pad_maximum_fusion.5), channel_id=1, replica_groups=mesh['groups'=2,'people'=4,'blocks'=2,'sub'=2] {'people','sub'}, use_global_device_ids=true, to_apply=%region_9.10 | all-reduce | flops 4192 | bytes 33536 | tf_op jit(solution)/shard_map/psum | solution.py:88
  49.0 58.6 %reduce-scatter.2.cloned.1.call-done = f32[2,128,1024]{2,1,0:T(8,128)} async-done(((f32[2,1024,1024]{2,1,0:T(8,128)}), f32[2,128,1024]{2,1,0:T(8,128)}) %reduce-scatter.2.cloned.1.call-update) | async-done | bytes 1048592 | tf_op jit(solution)/shard_map/reduce_scatter | solution.py:110
  107.6 1.7 multiply_divide_fusion.1
  109.3 1.2 pad_maximum_fusion.1
  110.5 0.5 broadcast.463
  111.0 0.8 reduce.4
  111.8 0.6 reshape.722
  112.4 3.8 %all-to-all-start.1 = ((bf16[4,2,1536]{2,1,0:T(2,128)(2,1)}), bf16[4,2,1536]{2,1,0:T(2,128)(2,1)S(1)}, u32[]{:S(2)}, u32[]{:S(2)}) async-start(bf16[4,2,1536]{2,1,0:T(2,128)(2,1)} %reshape.722), calls=%async_computation.2 | async-start | bytes 49152 | tf_op jit(solution)/shard_map/all_to_all | solution.py:144
  116.4 3.1 all-to-all-done.1
  119.6 44.7 %all-reduce.4.cloned.1.call-done = f32[2,1024,48]{1,2,0:T(8,128)} async-done(((f32[2,1024,48]{1,2,0:T(8,128)}), f32[2,1024,48]{1,2,0:T(8,128)}) %all-reduce.4.cloned.1.call-update) | async-done | bytes 393232 | tf_op jit(solution)/shard_map/psum | solution.py:88
  164.3 1.1 fusion.89
  165.9 81.2 %all-gather.2.cloned.1.call-done = f32[2,1024,1024]{2,1,0:T(8,128)} async-done(((f32[2,128,1024]{2,1,0:T(8,128)}), f32[2,1024,1024]{2,1,0:T(8,128)}) %all-gather.2.cloned.1.call-update) | async-done | bytes 8388624 | tf_op jit(solution)/shard_map/all_gather | solution.py:114
  247.1 6.4 %multiply_reduce_fusion.17 = (f32[60]{0:T(128)S(1)}, f32[1024,60]{0,1:T(8,128)S(1)}) fusion(f32[1024,60]{0,1:T(8,128)S(1)} %tile.16, f32[60]{0:T(128)S(1)} %mul.733, f32[2,1024,1024]{2,1,0:T(8,128)} %all-gather.2.cloned.1.call-done, s32[]{:T(128)S(6)} %select_n.49), kind=kOutput, calls=%fused_computation.123 | convolution fusion | flops 755220416 | bytes 4965108 | tf_op jit(solution)/shard_map/dot_general | solution.py:123
  253.9 6.5 %multiply_reduce_fusion.15 = (f32[60]{0:T(128)S(1)}, f32[1024,60]{0,1:T(8,128)S(1)}) fusion(f32[1024,60]{0,1:T(8,128)S(1)} %multiply_add_fusion.10, f32[60]{0:T(128)S(1)} %mul.733, f32[2,1024,1024]{2,1,0:T(8,128)} %all-gather.2.cloned.1.call-done, s32[]{:T(128)S(6)} %select_n.49), kind=kOutput, calls=%fused_computation.119 | convolution fusion | flops 755220416 | bytes 4965108 | tf_op jit(solution)/shard_map/dot_general | solution.py:123
  260.7 6.5 %multiply_reduce_fusion.13 = (f32[60]{0:T(128)S(1)}, f32[1024,60]{0,1:T(8,128)S(1)}) fusion(f32[1024,60]{0,1:T(8,128)S(1)} %multiply_add_fusion.9, f32[60]{0:T(128)S(1)} %mul.733, f32[2,1024,1024]{2,1,0:T(8,128)} %all-gather.2.cloned.1.call-done, s32[]{:T(128)S(6)} %select_n.49), kind=kOutput, calls=%fused_computation.115 | convolution fusion | flops 755220416 | bytes 4965108 | tf_op jit(solution)/shard_map/dot_general | solution.py:123
  267.5 6.6 %multiply_reduce_fusion.11 = (f32[60]{0:T(128)S(1)}, f32[1024,60]{0,1:T(8,128)S(1)}) fusion(f32[1024,60]{0,1:T(8,128)S(1)} %multiply_add_fusion.8, f32[60]{0:T(128)S(1)} %mul.733, f32[2,1024,1024]{2,1,0:T(8,128)} %all-gather.2.cloned.1.call-done, s32[]{:T(128)S(6)} %select_n.49), kind=kOutput, calls=%fused_computation.111 | convolution fusion | flops 755220416 | bytes 4965108 | tf_op jit(solution)/shard_map/dot_general | solution.py:123
  274.5 6.5 %multiply_reduce_fusion.9 = (f32[60]{0:T(128)S(1)}, f32[1024,60]{0,1:T(8,128)S(1)}) fusion(f32[1024,60]{0,1:T(8,128)S(1)} %multiply_add_fusion.7, f32[60]{0:T(128)S(1)} %mul.733, f32[2,1024,1024]{2,1,0:T(8,128)} %all-gather.2.cloned.1.call-done, s32[]{:T(128)S(6)} %select_n.49), kind=kOutput, calls=%fused_computation.107 | convolution fusion | flops 755220416 | bytes 4965108 | tf_op jit(solution)/shard_map/dot_general | solution.py:123
  281.3 6.5 %multiply_reduce_fusion.7 = (f32[60]{0:T(128)S(1)}, f32[1024,60]{0,1:T(8,128)S(1)}) fusion(f32[1024,60]{0,1:T(8,128)S(1)} %multiply_add_fusion.6, f32[60]{0:T(128)S(1)} %mul.733, f32[2,1024,1024]{2,1,0:T(8,128)} %all-gather.2.cloned.1.call-done, s32[]{:T(128)S(6)} %select_n.49), kind=kOutput, calls=%fused_computation.103 | convolution fusion | flops 755220416 | bytes 4965108 | tf_op jit(solution)/shard_map/dot_general | solution.py:123
  288.2 6.6 %multiply_reduce_fusion.5 = (f32[60]{0:T(128)S(1)}, f32[1024,60]{0,1:T(8,128)S(1)}) fusion(f32[1024,60]{0,1:T(8,128)S(1)} %multiply_add_fusion.5, f32[60]{0:T(128)S(1)} %mul.733, f32[2,1024,1024]{2,1,0:T(8,128)} %all-gather.2.cloned.1.call-done, s32[]{:T(128)S(6)} %select_n.49), kind=kOutput, calls=%fused_computation.99 | convolution fusion | flops 755220416 | bytes 4965108 | tf_op jit(solution)/shard_map/dot_general | solution.py:123
  295.1 6.8 %multiply_reduce_fusion.3 = (f32[60]{0:T(128)S(1)}, f32[1024,60]{0,1:T(8,128)S(1)}) fusion(f32[1024,60]{0,1:T(8,128)S(1)} %multiply_add_fusion.4, f32[60]{0:T(128)S(1)} %mul.733, f32[2,1024,1024]{2,1,0:T(8,128)} %all-gather.2.cloned.1.call-done, s32[]{:T(128)S(6)} %select_n.49), kind=kOutput, calls=%fused_computation.95 | convolution fusion | flops 755220416 | bytes 4965108 | tf_op jit(solution)/shard_map/dot_general | solution.py:123
  302.3 6.5 %multiply_reduce_fusion.1 = (f32[60]{0:T(128)S(1)}, f32[1024,60]{0,1:T(8,128)S(1)}) fusion(f32[1024,60]{0,1:T(8,128)S(1)} %multiply_add_fusion.3, f32[60]{0:T(128)S(1)} %mul.733, f32[2,1024,1024]{2,1,0:T(8,128)} %all-gather.2.cloned.1.call-done, s32[]{:T(128)S(6)} %select_n.49), kind=kOutput, calls=%fused_computation.91 | convolution fusion | flops 755220416 | bytes 4965108 | tf_op jit(solution)/shard_map/dot_general | solution.py:123
  309.0 4.3 %fusion.67 = f32[60]{0:T(128)S(1)} fusion(f32[2,1024,1024]{2,1,0:T(8,128)S(1)} %bitcast.162, s32[]{:T(128)S(6)} %select_n.49, f32[1024,60]{0,1:T(8,128)S(1)} %get-tuple-element.23, f32[1024,60]{0,1:T(8,128)S(1)} %multiply_add_fusion.3, f32[60]{0:T(128)S(1)} %div.291, f32[60]{0:T(128)S(1)} %mul.733), kind=kOutput, calls=%fused_computation.56 | convolution fusion | flops 755466176 | bytes 5244660 | tf_op jit(solution)/shard_map/dot_general | solution.py:123
  313.7 17.7 %all_gather.7 = bf16[8,1024,5,12]{1,3,2,0:T(8,128)(2,1)S(1)} all-gather(bf16[1,1024,5,12]{1,3,2,0:T(8,128)(2,1)S(1)} %broadcast_in_dim_reshape.2), channel_id=1, replica_groups=mesh['groups'=2,'people'=4,'blocks'=2,'sub'=2] {'people','sub'}, dimensions={0}, use_global_device_ids=true | all-gather | bytes 1105920 | tf_op jit(solution)/shard_map/all_gather | solution.py:129
  331.3 1.0 copy.84
  332.4 1.7 fusion.149
  334.1 0.5 copy.54
  334.8 0.5 fusion.124
  335.2 0.6 copy.55
  335.9 0.5 fusion.122
  336.4 0.4 fusion.65
  336.8 0.3 fusion.66
  337.1 0.7 copy.56
  337.8 3.4 all-to-all-start
  341.4 5.1 %all-to-all-done = bf16[1,256,5,48]{1,2,0,3:T(8,128)(2,1)S(1)} async-done(((bf16[1,256,5,48]{1,2,0,3:T(8,128)(2,1)}), bf16[1,256,5,48]{1,2,0,3:T(8,128)(2,1)S(1)}, u32[]{:S(2)}, u32[]{:S(2)}) %all-to-all-start) | async-done | bytes 122912 | tf_op jit(solution)/shard_map/all_to_all | solution.py:143
  347.1 18.9 %all-reduce.1 = (f32[12,10,10]{2,1,0:T(8,128)S(1)}, f32[12,10]{1,0:T(8,128)S(1)}) all-reduce(f32[12,10,10]{2,1,0:T(8,128)S(1)} %fusion.94, f32[12,10]{1,0:T(8,128)S(1)} %bitcast.176), channel_id=1, replica_groups=mesh['groups'=2,'people'=4,'blocks'=2,'sub'=2] {'people'}, use_global_device_ids=true, to_apply=%region_33.34 | all-reduce | flops 1320 | bytes 10560 | tf_op jit(solution)/shard_map/psum | solution.py:160
  366.4 0.4 multiply_reduce_fusion.23
  367.1 0.4 multiply_reduce_fusion.21
  367.8 0.4 multiply_reduce_fusion.19
  368.4 0.4 fusion.71
  368.8 0.3 fusion.90
  369.1 0.7 copy.65
  (101 shorter events, 7.0 us)
Async XLA Ops:
  6.5 101.0 %reduce-scatter.2.cloned.1.call-start = ((), (), s32[]{:S(2)}) async-start(), calls=%async_computation.4 | async-start | bytes 9437184 | tf_op jit(solution)/shard_map/reduce_scatter | solution.py:110
  14.6 0.7 copy-start
  14.7 101.6 %copy-start.1 = (f32[5]{0:T(128)S(1)}, f32[5]{0:T(128)}, u32[]{:S(2)}) copy-start(f32[5]{0:T(128)} %param.7) | copy-start | bytes 64
  14.7 149.7 %all-reduce.4.cloned.1.call-start = ((), (), s32[]{:S(2)}) async-start(), calls=%async_computation.3 | async-start | bytes 786432 | tf_op jit(solution)/shard_map/psum | solution.py:88
  16.7 230.3 %all-gather.2.cloned.1.call-start = ((), (), s32[]{:S(2)}) async-start(), calls=%async_computation.5 | async-start | bytes 9437184 | tf_op jit(solution)/shard_map/all_gather | solution.py:114
  112.4 7.1 %all-to-all-start.1 = ((bf16[4,2,1536]{2,1,0:T(2,128)(2,1)}), bf16[4,2,1536]{2,1,0:T(2,128)(2,1)S(1)}, u32[]{:S(2)}, u32[]{:S(2)}) async-start(bf16[4,2,1536]{2,1,0:T(2,128)(2,1)} %reshape.722), calls=%async_computation.2 | async-start | bytes 49152 | tf_op jit(solution)/shard_map/all_to_all | solution.py:144
  288.1 20.9 %slice-start = ((s8[8388608]{0:T(1024)(128)(4,1)}), s8[4194304]{0:T(1024)(128)(4,1)S(1)}, s32[]{:S(2)}) async-start(s8[8388608]{0:T(1024)(128)(4,1)} %bitcast.161), calls=%async_computation.6 | async-start | bytes 8388608
  295.1 13.9 %slice-start.1 = ((s8[8388608]{0:T(1024)(128)(4,1)}), s8[4194304]{0:T(1024)(128)(4,1)S(1)}, s32[]{:S(2)}) async-start(s8[8388608]{0:T(1024)(128)(4,1)} %bitcast.161), calls=%async_computation.7 | async-start | bytes 8388608
  337.8 8.6 %all-to-all-start = ((bf16[1,256,5,48]{1,2,0,3:T(8,128)(2,1)}), bf16[1,256,5,48]{1,2,0,3:T(8,128)(2,1)S(1)}, u32[]{:S(2)}, u32[]{:S(2)}) async-start(bf16[1,256,5,48]{1,2,0,3:T(8,128)(2,1)} %copy.56), calls=%async_computation.1 | async-start | bytes 393216 | tf_op jit(solution)/shard_map/all_to_all | solution.py:143
Sparse Core Ops, SparseCore 0:
  14.8 92.7 reduce-scatter.1
  109.9 54.3 all-reduce.3
  166.0 81.0 all-gather.1
where the time goes:
time: 381 us; the launch traced here: 377 us
  waiting for transfers between devices  193 us (51%)
  matrix products  69.3 us (18%)
  blocking collectives  68.3 us (18%)
  other arithmetic  16.9 us (4%)
  between operations  14 us (4%)
  local copies, waits for them, and re-layouts  8.12 us (2%)
  starting transfers between devices  7.23 us (2%)
    all_gather x1, waiting for transfers between devices, shards(): whole = lax.all_gather(systems, ('people', 'sub'), axis=1, tiled=True)  81.2 us
    dot_general x10, matrix products, shards(): jnp.dot(system, direction, precision=highest) + shifts * direction  63.1 us
    reduce_scatter x1, waiting for transfers between devices, shards(): lax.psum_scatter(gram_stack, ('people', 'sub'), scatter_dimension=1, tile...  58.6 us
    psum x1, waiting for transfers between devices, shards(): lax.psum((jnp.stack(sums), jnp.stack(squares), jnp.stack(cross), jnp.stac...  44.7 us
    psum x1, blocking collectives, shards(): lax.psum((jnp.stack(sums), jnp.stack(squares), jnp.stack(cross), jnp.stac...  31.8 us
    psum x1, blocking collectives, shards(): gram_two, cross_two = lax.psum((gram_two, cross_two), 'people')  18.9 us
    all_gather x1, blocking collectives, shards(): lax.all_gather(scaled[None], ('people', 'sub'), axis=0, tiled=True)  17.7 us
  transfers between devices with their start and end apart: 5, of which 5 were waited for; matrix products, arithmetic and copies ran while one was open for 2% of the time, Pallas kernels for 0%

commit v1 on v0

--- a/solution.py
+++ b/solution.py
@@ -9,6 +9,12 @@
 ITERS = 10
 ITERS_TWO = 4
 highest = lax.Precision.HIGHEST
+
+
+def in_order(blocks, dim):
+    lengths = list(blocks.shape[1:])
+    lengths[dim] *= blocks.shape[0]
+    return jnp.moveaxis(blocks, 0, dim).reshape(lengths)
 
 
 def conjugate(apply_system, right_side, steps):
@@ -111,7 +117,19 @@
     systems, row_spread = system_rows(
         shares, sums_all, column_mean, column_spread, row_start, share_rows, train_count
     )
-    whole = lax.all_gather(systems, ("people", "sub"), axis=1, tiled=True)
+    length = lax.axis_size(("people", "sub"))
+    pairs = [(i, (i + 1) % length) for i in range(length)]
+    back = [(b, a) for a, b in pairs]
+    lower, upper = ([], [])
+    for k in range(length - 1):
+        if k % 2 == 0:
+            lower.append(lax.ppermute(lower[-1] if lower else systems, ("people", "sub"), pairs))
+        else:
+            upper.append(lax.ppermute(upper[-1] if upper else systems, ("people", "sub"), back))
+    tiles = jnp.stack([*lower[::-1], systems, *upper])
+    shift = lax.axis_index(("people", "sub")) - len(lower)
+    tiles = tiles[(jnp.arange(length) - shift) % length]
+    whole = in_order(tiles, 1)
     own_fold = lax.axis_index("sub")
     system = lax.dynamic_index_in_dim(whole, own_fold, 0, keepdims=False)
     trait_share = TRAITS // people_count

time: 381 us -> 395 us (1.037)
  local copies, waits for them, and re-layouts: 8.12 us -> 34.6 us
  waiting for transfers between devices: 193 us -> 176 us
  starting transfers between devices: 7.23 us -> 14.1 us
  matrix products: 69.3 us -> 65.2 us
    all_gather x1 -> x0, waiting for transfers between devices: 81.2 us -> none  [shards(): whole = lax.all_gather(systems, ('people', 'sub'), axis=1, tiled=True)]
    ppermute x0 -> x7, waiting for transfers between devices: none -> 57.7 us  [the longest x4 57.7 us: shards(): lax.ppermute(lower[-1] if lower else systems, ('people', 'sub'), pairs)]
    unnamed x11 -> x21, local copies, waits for them, and re-layouts: 1.83 us -> 15.6 us
    gather x0 -> x1, local copies, waits for them, and re-layouts: none -> 7.67 us  [shards(): tiles = tiles[(jnp.arange(length) - shift) % length]]
    ppermute x0 -> x7, starting transfers between devices: none -> 7.44 us  [the longest x3 7.37 us: shards(): lax.ppermute(upper[-1] if upper else systems, ('people', 'sub'), back)]
    psum x1, waiting for transfers between devices: 44.7 us -> 49.8 us  [shards(): lax.psum((jnp.stack(sums), jnp.stack(squares), jnp.stack(cross), jnp.stac...]
    transpose x0 -> x1, local copies, waits for them, and re-layouts: none -> 4.23 us  [in_order(): return jnp.moveaxis(blocks, 0, dim).reshape(lengths)]
    dot_general x10, matrix products: 63.1 us -> 59 us  [shards(): jnp.dot(system, direction, precision=highest) + shifts * direction]
  transfers between devices with their start and end apart: 5 -> 11, of which waited for: 5 -> 7; matrix products, arithmetic and copies ran while one was open for 2% -> 5% of each run, Pallas kernels for 0% -> 0%
where the time goes in v1:
time: 395 us; the launch traced here: 390 us
  waiting for transfers between devices  176 us (45%)
  blocking collectives  68.2 us (17%)
  matrix products  65.2 us (17%)
  local copies, waits for them, and re-layouts  34.6 us (9%)
  other arithmetic  16.9 us (4%)
  between operations  14.3 us (4%)
  starting transfers between devices  14.1 us (4%)
    reduce_scatter x1, waiting for transfers between devices, shards(): lax.psum_scatter(gram_stack, ('people', 'sub'), scatter_dimension=1, tile...  60.1 us
    dot_general x10, matrix products, shards(): jnp.dot(system, direction, precision=highest) + shifts * direction  59 us
    ppermute x4, waiting for transfers between devices, shards(): lax.ppermute(lower[-1] if lower else systems, ('people', 'sub'), pairs)  57.7 us
    psum x1, waiting for transfers between devices, shards(): lax.psum((jnp.stack(sums), jnp.stack(squares), jnp.stack(cross), jnp.stac...  49.8 us
    psum x1, blocking collectives, shards(): lax.psum((jnp.stack(sums), jnp.stack(squares), jnp.stack(cross), jnp.stac...  31.7 us
    psum x1, blocking collectives, shards(): gram_two, cross_two = lax.psum((gram_two, cross_two), 'people')  19.2 us
    all_gather x1, blocking collectives, shards(): lax.all_gather(scaled[None], ('people', 'sub'), axis=0, tiled=True)  17.4 us
    unnamed x21, local copies, waits for them, and re-layouts  15.6 us
  transfers between devices with their start and end apart: 11, of which 7 were waited for; matrix products, arithmetic and copies ran while one was open for 5% of the time, Pallas kernels for 0%

profile of v1, /device:TPU:0, one launch (start us, length us, event | category | flops | bytes accessed | tf_op | source)
XLA Modules:
  0.0 389.6 jit_solution(16224117206466757311)
XLA Ops:
  6.5 0.7 broadcast_compare_fusion
  7.2 1.7 convert_reduce_fusion.1
  8.9 0.8 convolution_bitcast_fusion
  9.7 0.8 convolution_bitcast_fusion.1
  10.6 4.1 %pad_maximum_fusion = f32[2,1024,1024]{2,1,0:T(8,128)} fusion(f32[1,1024,1024]{2,1,0:T(8,128)S(1)} %convolution_bitcast_fusion, f32[1,1024,1024]{2,1,0:T(8,128)S(1)} %convolution_bitcast_fusion.1), kind=kLoop, calls=%fused_computation.1 | loop fusion | flops 2097152 | bytes 16777216 | tf_op jit(solution)/shard_map/stack | solution.py:113
  15.5 31.7 %all-reduce = (f32[2,1024]{1,0:T(2,128)S(1)}, f32[2,1024]{1,0:T(2,128)S(1)}, f32[2,48]{1,0:T(2,128)S(1)}) all-reduce(f32[2,1024]{1,0:T(2,128)S(1)} %get-tuple-element.88, f32[2,1024]{1,0:T(2,128)S(1)} %get-tuple-element.87, f32[2,48]{1,0:T(2,128)S(1)} %pad_maximum_fusion.5), channel_id=1, replica_groups=mesh['groups'=2,'people'=4,'blocks'=2,'sub'=2] {'people','sub'}, use_global_device_ids=true, to_apply=%region_9.10 | all-reduce | flops 4192 | bytes 33536 | tf_op jit(solution)/shard_map/psum | solution.py:94
  47.4 60.1 %reduce-scatter.2.cloned.1.call-done = f32[2,128,1024]{2,1,0:T(8,128)} async-done(((f32[2,1024,1024]{2,1,0:T(8,128)}), f32[2,128,1024]{2,1,0:T(8,128)}) %reduce-scatter.2.cloned.1.call-update) | async-done | bytes 1048592 | tf_op jit(solution)/shard_map/reduce_scatter | solution.py:116
  107.6 1.7 multiply_divide_fusion.1
  109.4 16.0 %collective-permute-done = f32[2,128,1024]{2,1,0:T(8,128)S(1)} collective-permute-done((f32[2,128,1024]{2,1,0:T(8,128)S(1)}, f32[2,128,1024]{2,1,0:T(8,128)S(1)}, u32[]{:S(2)}, u32[]{:S(2)}) %collective-permute-start) | collective-permute-done | bytes 1048608 | tf_op jit(solution)/shard_map/ppermute | solution.py:126
  125.4 3.5 collective-permute-start.4
  129.0 21.4 %collective-permute-done.1 = f32[2,128,1024]{2,1,0:T(8,128)S(1)} collective-permute-done((f32[2,128,1024]{2,1,0:T(8,128)S(1)}, f32[2,128,1024]{2,1,0:T(8,128)S(1)}, u32[]{:S(2)}, u32[]{:S(2)}) %collective-permute-start.1) | collective-permute-done | bytes 1048608 | tf_op jit(solution)/shard_map/ppermute | solution.py:126
  150.3 1.0 copy-done.1
  151.9 3.6 collective-permute-start.5
  155.5 20.3 %collective-permute-done.2 = f32[2,128,1024]{2,1,0:T(8,128)} collective-permute-done((f32[2,128,1024]{2,1,0:T(8,128)S(1)}, f32[2,128,1024]{2,1,0:T(8,128)}, u32[]{:S(2)}, u32[]{:S(2)}) %collective-permute-start.2) | collective-permute-done | bytes 1048608 | tf_op jit(solution)/shard_map/ppermute | solution.py:126
  175.8 0.8 pad_maximum_fusion.2
  177.2 0.8 reduce.4
  178.6 3.3 all-to-all-start.1
  182.1 3.6 all-to-all-done.1
  185.7 49.8 %all-reduce.4.cloned.1.call-done = f32[2,1024,48]{1,2,0:T(8,128)} async-done(((f32[2,1024,48]{1,2,0:T(8,128)}), f32[2,1024,48]{1,2,0:T(8,128)}) %all-reduce.4.cloned.1.call-update) | async-done | bytes 393232 | tf_op jit(solution)/shard_map/psum | solution.py:94
  235.5 1.1 fusion.89
  237.3 2.3 bitcast_dynamic-update-slice_fusion.7
  239.6 2.4 bitcast_dynamic-update-slice_fusion.6
  242.0 2.3 bitcast_dynamic-update-slice_fusion.5
  244.3 1.1 bitcast_dynamic-update-slice_fusion.4
  245.3 1.0 bitcast_dynamic-update-slice_fusion.3
  246.4 2.4 bitcast_dynamic-update-slice_fusion.2
  248.7 2.3 bitcast_dynamic-update-slice_fusion.1
  251.1 1.1 bitcast_dynamic-update-slice_fusion
  252.2 7.7 %gather_fusion = f32[8,2,128,1024]{3,2,1,0:T(8,128)} fusion(f32[8,2,128,1024]{3,2,1,0:T(8,128)} %bitcast_dynamic-update-slice_fusion, s32[1024]{0:T(1024)S(1)} %pad_clamp_fusion), kind=kCustom, calls=%fused_computation | custom fusion | bytes 16777248 | tf_op jit(solution)/shard_map/gather | solution.py:131
  259.8 4.2 %copy.57 = f32[2,8,128,1024]{3,2,1,0:T(8,128)S(1)} copy(f32[2,8,128,1024]{3,2,0,1:T(8,128)} %bitcast.193) | data formatting | bytes 16777216 | tf_op jit(solution)/shard_map/transpose | solution.py:17
  264.1 4.3 %multiply_reduce_fusion.17 = (f32[60]{0:T(128)S(1)}, f32[1024,60]{0,1:T(8,128)S(1)}) fusion(f32[1024,60]{0,1:T(8,128)S(1)} %tile.16, f32[60]{0:T(128)S(1)} %mul.734, f32[2,1024,1024]{2,1,0:T(8,128)S(1)} %bitcast.181, s32[]{:T(128)S(6)} %select_n.73), kind=kOutput, calls=%fused_computation.132 | convolution fusion | flops 755220416 | bytes 4965108 | tf_op jit(solution)/shard_map/dot_general | solution.py:141
  268.7 4.3 %multiply_reduce_fusion.15 = (f32[60]{0:T(128)S(1)}, f32[1024,60]{0,1:T(8,128)S(1)}) fusion(f32[1024,60]{0,1:T(8,128)S(1)} %multiply_add_fusion.10, f32[60]{0:T(128)S(1)} %mul.734, f32[2,1024,1024]{2,1,0:T(8,128)S(1)} %bitcast.182, s32[]{:T(128)S(6)} %select_n.73), kind=kOutput, calls=%fused_computation.128 | convolution fusion | flops 755220416 | bytes 4965108 | tf_op jit(solution)/shard_map/dot_general | solution.py:141
  273.4 6.5 %multiply_reduce_fusion.13 = (f32[60]{0:T(128)S(1)}, f32[1024,60]{0,1:T(8,128)S(1)}) fusion(f32[1024,60]{0,1:T(8,128)S(1)} %multiply_add_fusion.9, f32[60]{0:T(128)S(1)} %mul.734, f32[2,1024,1024]{2,1,0:T(8,128)} %bitcast.183, s32[]{:T(128)S(6)} %select_n.73), kind=kOutput, calls=%fused_computation.124 | convolution fusion | flops 755220416 | bytes 4965108 | tf_op jit(solution)/shard_map/dot_general | solution.py:141
  280.2 6.7 %multiply_reduce_fusion.11 = (f32[60]{0:T(128)S(1)}, f32[1024,60]{0,1:T(8,128)S(1)}) fusion(f32[1024,60]{0,1:T(8,128)S(1)} %multiply_add_fusion.8, f32[60]{0:T(128)S(1)} %mul.734, f32[2,1024,1024]{2,1,0:T(8,128)} %bitcast.184, s32[]{:T(128)S(6)} %select_n.73), kind=kOutput, calls=%fused_computation.120 | convolution fusion | flops 755220416 | bytes 4965108 | tf_op jit(solution)/shard_map/dot_general | solution.py:141
  287.2 6.5 %multiply_reduce_fusion.9 = (f32[60]{0:T(128)S(1)}, f32[1024,60]{0,1:T(8,128)S(1)}) fusion(f32[1024,60]{0,1:T(8,128)S(1)} %multiply_add_fusion.7, f32[60]{0:T(128)S(1)} %mul.734, f32[2,1024,1024]{2,1,0:T(8,128)} %bitcast.185, s32[]{:T(128)S(6)} %select_n.73), kind=kOutput, calls=%fused_computation.116 | convolution fusion | flops 755220416 | bytes 4965108 | tf_op jit(solution)/shard_map/dot_general | solution.py:141
  294.1 6.5 %multiply_reduce_fusion.7 = (f32[60]{0:T(128)S(1)}, f32[1024,60]{0,1:T(8,128)S(1)}) fusion(f32[1024,60]{0,1:T(8,128)S(1)} %multiply_add_fusion.6, f32[60]{0:T(128)S(1)} %mul.734, f32[2,1024,1024]{2,1,0:T(8,128)} %bitcast.186, s32[]{:T(128)S(6)} %select_n.73), kind=kOutput, calls=%fused_computation.112 | convolution fusion | flops 755220416 | bytes 4965108 | tf_op jit(solution)/shard_map/dot_general | solution.py:141
  300.9 7.0 %multiply_reduce_fusion.5 = (f32[60]{0:T(128)S(1)}, f32[1024,60]{0,1:T(8,128)S(1)}) fusion(f32[1024,60]{0,1:T(8,128)S(1)} %multiply_add_fusion.5, f32[60]{0:T(128)S(1)} %mul.734, f32[2,1024,1024]{2,1,0:T(8,128)} %bitcast.187, s32[]{:T(128)S(6)} %select_n.73), kind=kOutput, calls=%fused_computation.108 | convolution fusion | flops 755220416 | bytes 4965108 | tf_op jit(solution)/shard_map/dot_general | solution.py:141
  308.3 6.6 %multiply_reduce_fusion.3 = (f32[60]{0:T(128)S(1)}, f32[1024,60]{0,1:T(8,128)S(1)}) fusion(f32[1024,60]{0,1:T(8,128)S(1)} %multiply_add_fusion.4, f32[60]{0:T(128)S(1)} %mul.734, f32[2,1024,1024]{2,1,0:T(8,128)} %bitcast.188, s32[]{:T(128)S(6)} %select_n.73), kind=kOutput, calls=%fused_computation.104 | convolution fusion | flops 755220416 | bytes 4965108 | tf_op jit(solution)/shard_map/dot_general | solution.py:141
  315.2 6.5 %multiply_reduce_fusion.1 = (f32[60]{0:T(128)S(1)}, f32[1024,60]{0,1:T(8,128)S(1)}) fusion(f32[1024,60]{0,1:T(8,128)S(1)} %multiply_add_fusion.3, f32[60]{0:T(128)S(1)} %mul.734, f32[2,1024,1024]{2,1,0:T(8,128)} %bitcast.189, s32[]{:T(128)S(6)} %select_n.73), kind=kOutput, calls=%fused_computation.100 | convolution fusion | flops 755220416 | bytes 4965108 | tf_op jit(solution)/shard_map/dot_general | solution.py:141
  322.0 4.3 %fusion.67 = f32[60]{0:T(128)S(1)} fusion(f32[2,1024,1024]{2,1,0:T(8,128)S(1)} %bitcast.192, s32[]{:T(128)S(6)} %select_n.73, f32[1024,60]{0,1:T(8,128)S(1)} %get-tuple-element.23, f32[1024,60]{0,1:T(8,128)S(1)} %multiply_add_fusion.3, f32[60]{0:T(128)S(1)} %div.291, f32[60]{0:T(128)S(1)} %mul.734), kind=kOutput, calls=%fused_computation.57 | convolution fusion | flops 755466176 | bytes 5244660 | tf_op jit(solution)/shard_map/dot_general | solution.py:141
  326.6 17.4 %all_gather.3 = bf16[8,1024,5,12]{1,3,2,0:T(8,128)(2,1)S(1)} all-gather(bf16[1,1024,5,12]{1,3,2,0:T(8,128)(2,1)S(1)} %broadcast_in_dim_reshape.2), channel_id=1, replica_groups=mesh['groups'=2,'people'=4,'blocks'=2,'sub'=2] {'people','sub'}, dimensions={0}, use_global_device_ids=true | all-gather | bytes 1105920 | tf_op jit(solution)/shard_map/all_gather | solution.py:147
  344.0 1.0 copy.89
  345.0 1.5 fusion.151
  349.5 0.7 copy.61
  350.2 3.4 all-to-all-start
  353.8 5.1 %all-to-all-done = bf16[1,256,5,48]{1,2,0,3:T(8,128)(2,1)S(1)} async-done(((bf16[1,256,5,48]{1,2,0,3:T(8,128)(2,1)}), bf16[1,256,5,48]{1,2,0,3:T(8,128)(2,1)S(1)}, u32[]{:S(2)}, u32[]{:S(2)}) %all-to-all-start) | async-done | bytes 122912 | tf_op jit(solution)/shard_map/all_to_all | solution.py:161
  359.5 19.2 %all-reduce.1 = (f32[12,10,10]{2,1,0:T(8,128)S(1)}, f32[12,10]{1,0:T(8,128)S(1)}) all-reduce(f32[12,10,10]{2,1,0:T(8,128)S(1)} %fusion.94, f32[12,10]{1,0:T(8,128)S(1)} %bitcast.207), channel_id=1, replica_groups=mesh['groups'=2,'people'=4,'blocks'=2,'sub'=2] {'people'}, use_global_device_ids=true, to_apply=%region_33.34 | all-reduce | flops 1320 | bytes 10560 | tf_op jit(solution)/shard_map/psum | solution.py:178
  381.8 0.7 copy.70
  (128 shorter events, 13.9 us)
Async XLA Ops:
  6.5 101.1 %reduce-scatter.2.cloned.1.call-start = ((), (), s32[]{:S(2)}) async-start(), calls=%async_computation.4 | async-start | bytes 9437184 | tf_op jit(solution)/shard_map/reduce_scatter | solution.py:116
  14.6 0.7 copy-start.2
  14.6 167.3 %copy-start.3 = (f32[5]{0:T(128)S(1)}, f32[5]{0:T(128)}, u32[]{:S(2)}) copy-start(f32[5]{0:T(128)} %param.7) | copy-start | bytes 64
  14.7 220.8 %all-reduce.4.cloned.1.call-start = ((), (), s32[]{:S(2)}) async-start(), calls=%async_computation.3 | async-start | bytes 786432 | tf_op jit(solution)/shard_map/psum | solution.py:94
  109.4 16.1 %collective-permute-start = (f32[2,128,1024]{2,1,0:T(8,128)S(1)}, f32[2,128,1024]{2,1,0:T(8,128)S(1)}, u32[]{:S(2)}, u32[]{:S(2)}) collective-permute-start(f32[2,128,1024]{2,1,0:T(8,128)S(1)} %pad_maximum_fusion.1), channel_id=1, source_target_pairs={{0,1},{1,4},{4,5},{5,8},{8,9},{9,12},{12,13},{13,0},{2,3},{3,6},{6... | collective-permute-start | bytes 3145736 | tf_op jit(solution)/shard_map/ppermute | solution.py:126
  125.4 24.9 %collective-permute-start.1 = (f32[2,128,1024]{2,1,0:T(8,128)S(1)}, f32[2,128,1024]{2,1,0:T(8,128)S(1)}, u32[]{:S(2)}, u32[]{:S(2)}) collective-permute-start(f32[2,128,1024]{2,1,0:T(8,128)S(1)} %collective-permute-done), channel_id=1, source_target_pairs={{0,1},{1,4},{4,5},{5,8},{8,9},{9,12},{12,13},{13,0},{2,3},{3,6},{6... | collective-permute-start | bytes 3145736 | tf_op jit(solution)/shard_map/ppermute | solution.py:126
  125.4 26.4 %collective-permute-start.4 = (f32[2,128,1024]{2,1,0:T(8,128)S(1)}, f32[2,128,1024]{2,1,0:T(8,128)}, u32[]{:S(2)}, u32[]{:S(2)}) collective-permute-start(f32[2,128,1024]{2,1,0:T(8,128)S(1)} %pad_maximum_fusion.1), channel_id=1, source_target_pairs={{1,0},{4,1},{5,4},{8,5},{9,8},{12,9},{13,12},{0,13},{3,2},{6,3},{7... | collective-permute-start | bytes 3145736 | tf_op jit(solution)/shard_map/ppermute | solution.py:128
  150.3 1.0 copy-start.1
  151.3 24.5 %collective-permute-start.2 = (f32[2,128,1024]{2,1,0:T(8,128)S(1)}, f32[2,128,1024]{2,1,0:T(8,128)}, u32[]{:S(2)}, u32[]{:S(2)}) collective-permute-start(f32[2,128,1024]{2,1,0:T(8,128)S(1)} %collective-permute-done.1), channel_id=1, source_target_pairs={{0,1},{1,4},{4,5},{5,8},{8,9},{9,12},{12,13},{13,0},{2,3},{3,6},{6... | collective-permute-start | bytes 3145736 | tf_op jit(solution)/shard_map/ppermute | solution.py:126
  151.9 85.1 %collective-permute-start.5 = (f32[2,128,1024]{2,1,0:T(8,128)}, f32[2,128,1024]{2,1,0:T(8,128)}, u32[]{:S(2)}, u32[]{:S(2)}) collective-permute-start(f32[2,128,1024]{2,1,0:T(8,128)} %collective-permute-done.4), channel_id=1, source_target_pairs={{1,0},{4,1},{5,4},{8,5},{9,8},{12,9},{13,12},{0,13},{3,2},{6,3},{7... | collective-permute-start | bytes 3145736 | tf_op jit(solution)/shard_map/ppermute | solution.py:128
  175.8 61.4 %collective-permute-start.3 = (f32[2,128,1024]{2,1,0:T(8,128)}, f32[2,128,1024]{2,1,0:T(8,128)}, u32[]{:S(2)}, u32[]{:S(2)}) collective-permute-start(f32[2,128,1024]{2,1,0:T(8,128)} %collective-permute-done.2), channel_id=1, source_target_pairs={{0,1},{1,4},{4,5},{5,8},{8,9},{9,12},{12,13},{13,0},{2,3},{3,6},{6... | collective-permute-start | bytes 3145736 | tf_op jit(solution)/shard_map/ppermute | solution.py:126
  178.6 7.1 %all-to-all-start.1 = ((bf16[4,2,1536]{2,1,0:T(2,128)(2,1)}), bf16[4,2,1536]{2,1,0:T(2,128)(2,1)S(1)}, u32[]{:S(2)}, u32[]{:S(2)}) async-start(bf16[4,2,1536]{2,1,0:T(2,128)(2,1)} %reshape.783), calls=%async_computation.2 | async-start | bytes 49152 | tf_op jit(solution)/shard_map/all_to_all | solution.py:162
  237.0 14.1 %collective-permute-start.6 = (f32[2,128,1024]{2,1,0:T(8,128)}, f32[2,128,1024]{2,1,0:T(8,128)S(1)}, u32[]{:S(2)}, u32[]{:S(2)}) collective-permute-start(f32[2,128,1024]{2,1,0:T(8,128)} %collective-permute-done.5), channel_id=1, source_target_pairs={{1,0},{4,1},{5,4},{8,5},{9,8},{12,9},{13,12},{0,13},{3,2},{6,3},{7... | collective-permute-start | bytes 3145736 | tf_op jit(solution)/shard_map/ppermute | solution.py:128
  264.1 9.3 %copy-start = (f32[2,8,128,1024]{3,2,1,0:T(8,128)}, f32[2,8,128,1024]{3,2,1,0:T(8,128)S(1)}, u32[]{:S(2)}) copy-start(f32[2,8,128,1024]{3,2,1,0:T(8,128)S(1)} %copy.57) | copy-start | bytes 25165828
  300.9 21.1 %slice-start = ((s8[8388608]{0:T(1024)(128)(4,1)}), s8[4194304]{0:T(1024)(128)(4,1)S(1)}, s32[]{:S(2)}) async-start(s8[8388608]{0:T(1024)(128)(4,1)} %bitcast.190), calls=%async_computation.5 | async-start | bytes 8388608
  308.2 13.7 %slice-start.1 = ((s8[8388608]{0:T(1024)(128)(4,1)}), s8[4194304]{0:T(1024)(128)(4,1)S(1)}, s32[]{:S(2)}) async-start(s8[8388608]{0:T(1024)(128)(4,1)} %bitcast.190), calls=%async_computation.6 | async-start | bytes 8388608
  350.2 8.6 %all-to-all-start = ((bf16[1,256,5,48]{1,2,0,3:T(8,128)(2,1)}), bf16[1,256,5,48]{1,2,0,3:T(8,128)(2,1)S(1)}, u32[]{:S(2)}, u32[]{:S(2)}) async-start(bf16[1,256,5,48]{1,2,0,3:T(8,128)(2,1)} %copy.61), calls=%async_computation.1 | async-start | bytes 393216 | tf_op jit(solution)/shard_map/all_to_all | solution.py:161
Sparse Core Ops, SparseCore 0:
  14.8 92.7 reduce-scatter.1
  176.7 58.7 all-reduce.3
